TPU v7x, 128 devices: a whole 4x4x4 slice. The times are simulated.
128 devices in a mesh: sec: 2 (over y_lo), dp: 16 (over z, y_hi, core), tensor: 4 (over x).
Axes of the slice: x: 4, y: 4 (y_hi: 2, y_lo: 2; y = y_hi * 2 + y_lo), z: 4, core: 2. Of those that a mesh axis runs over, the one named last changes fastest.
Arguments:
- student_rows: bfloat16 [2, 8192, 5376], P('sec', 'dp'), may hold values from -24 to 24
- teacher_rows: bfloat16 [2, 8192, 5376], P('sec', 'dp'), may hold values from -6 to 6
- norm_gain: float32 [5376], replicated, may hold values from 0.5 to 1.5
- post_gain: float32 [5376], replicated, may hold values from 0.5 to 1.5
- query_weight: bfloat16 [5376, 2048], P(('sec', 'dp'), 'tensor')
- key_weight: bfloat16 [5376, 1024], P(('sec', 'dp'), 'tensor')
- value_weight: bfloat16 [5376, 1024], P(('sec', 'dp'), 'tensor'), may hold values from -0.078125 to 0.078125
- out_weight: bfloat16 [5376, 2048], P(('sec', 'dp'), 'tensor'), may hold values from -0.125 to 0.125
Outputs:
- layer_output: bfloat16 [2, 8192, 5376], P('sec', 'dp', 'tensor')
- query_grad: float32 [5376, 2048], P(('sec', 'dp'), 'tensor')
- output_grad: float32 [5376, 2048], P(('sec', 'dp'), 'tensor')
All inputs are finite; a program needn't handle non-finite values.
Results may differ from a plain program's by a relative error of at most 0.025.
The roundings to bfloat16 on the way count: a program that leaves them out, or rounds other values in their place, can miss the bound.
Values may be sent and summed in bfloat16 or wider, within the bound.
A program may use at most 128 MiB of HBM per device.

v0:
```python
import math
import jax
import jax.numpy as jnp
from jax import lax
from jax.sharding import PartitionSpec as P

HEADS = 8
KV_HEADS = 4
HD = 256
W = 1024
norm_eps = 1e-06
rope_base = 10000.0
masked_score = -1e30


def from_partner(block, axis, bit):
    count = lax.axis_size(axis)
    route = []
    for low in range(count):
        high = low | 1 << bit
        if high != low and high < count:
            route += [(low, high), (high, low)]
    return lax.ppermute(block, axis, route)


def from_behind(x, axis, by):
    count = lax.axis_size(axis)
    pairs = [(i, i + by) for i in range(count) if 0 <= i + by < count]
    return lax.ppermute(x, axis, pairs)


def rotate(values, cos_table, sin_table, sign_value):
    row_count = values.shape[0]
    half_dim = cos_table.shape[1]
    per_head = values.reshape(row_count, -1, 2 * half_dim)
    leading = per_head[:, :, :half_dim]
    trailing = per_head[:, :, half_dim:]
    cosines = cos_table[:, None, :]
    sin_scaled = sign_value * sin_table[:, None, :]
    rotated = jnp.concatenate(
        [leading * cosines - trailing * sin_scaled, trailing * cosines + leading * sin_scaled],
        axis=2,
    )
    return rotated.reshape(row_count, -1)


def shards(
    student_rows,
    teacher_rows,
    norm_gain,
    post_gain,
    query_weight,
    key_weight,
    value_weight,
    out_weight,
):
    tok_count = student_rows.shape[1]
    model_width = student_rows.shape[2]
    tensor_count = lax.axis_size("tensor")
    share_cols = model_width // tensor_count
    data_count = lax.axis_size("sec") * lax.axis_size("dp")
    blocks_back = (W + tok_count - 1) // tok_count
    key_count = (blocks_back + 1) * tok_count
    local_groups = key_weight.shape[1] // HD
    group_size = HEADS // KV_HEADS
    query_cols = query_weight.shape[1]
    score_scale = 1.0 / math.sqrt(HD)
    loss_scale = 2.0 / math.sqrt(data_count * tok_count)
    target = from_partner(teacher_rows[0], "sec", 0)
    query_full, key_full, value_full, out_full = (
        lax.all_gather(query_weight, ("sec", "dp"), axis=0, tiled=True),
        lax.all_gather(key_weight, ("sec", "dp"), axis=0, tiled=True),
        lax.all_gather(value_weight, ("sec", "dp"), axis=0, tiled=True),
        lax.all_gather(out_weight, ("sec", "dp"), axis=0, tiled=True),
    )
    student_f = student_rows[0].astype(jnp.float32)
    inverse = lax.rsqrt(jnp.mean(student_f * student_f, axis=1, keepdims=True) + norm_eps)
    normed = (student_f * inverse * norm_gain).astype(jnp.bfloat16)
    first_pos = lax.axis_index("dp") * tok_count
    half_dim = HD // 2
    inv_freq = jnp.power(
        jnp.float32(rope_base), -2.0 * jnp.arange(half_dim, dtype=jnp.float32) / HD
    )
    positions = (first_pos + jnp.arange(tok_count, dtype=jnp.int32)).astype(jnp.float32)
    angles = positions[:, None] * inv_freq[None, :]
    cos_table = jnp.cos(angles)
    sin_table = jnp.sin(angles)
    queries = rotate(
        jnp.dot(normed, query_full, preferred_element_type=jnp.float32), cos_table, sin_table, 1.0
    ).astype(jnp.bfloat16)
    key_rows = rotate(
        jnp.dot(normed, key_full, preferred_element_type=jnp.float32), cos_table, sin_table, 1.0
    ).astype(jnp.bfloat16)
    value_rows = jnp.dot(normed, value_full, preferred_element_type=jnp.float32).astype(
        jnp.bfloat16
    )
    key_parts = [key_rows]
    value_parts = [value_rows]
    for offset in range(1, blocks_back + 1):
        earlier_keys, earlier_values = from_behind((key_rows, value_rows), "dp", offset)
        key_parts = [earlier_keys] + key_parts
        value_parts = [earlier_values] + value_parts
    key_window = jnp.concatenate(key_parts, axis=0)
    value_window = jnp.concatenate(value_parts, axis=0)
    query_pos = first_pos + jnp.arange(tok_count, dtype=jnp.int32)
    key_pos = first_pos - blocks_back * tok_count + jnp.arange(key_count, dtype=jnp.int32)
    allowed = (
        (key_pos[None, :] >= 0)
        & (key_pos[None, :] <= query_pos[:, None])
        & (key_pos[None, :] > query_pos[:, None] - W)
    )
    grouped_q = queries.reshape(tok_count, local_groups, group_size, HD)
    grouped_k = key_window.reshape(key_count, local_groups, HD)
    grouped_v = value_window.reshape(key_count, local_groups, HD)
    scores = (
        jnp.einsum("tgad,kgd->gatk", grouped_q, grouped_k, preferred_element_type=jnp.float32)
        * score_scale
    )
    scores = jnp.where(allowed, scores, masked_score)
    row_peak = jnp.max(scores, axis=3, keepdims=True)
    exp_scores = jnp.exp(scores - row_peak)
    attn_probs = exp_scores / jnp.sum(exp_scores, axis=3, keepdims=True)
    probs_b = attn_probs.astype(jnp.bfloat16)
    mixed_rows = (
        jnp.einsum("gatk,kgd->tgad", probs_b, grouped_v, preferred_element_type=jnp.float32)
        .astype(jnp.bfloat16)
        .reshape(tok_count, query_cols)
    )
    partial_value = jnp.einsum(
        "te,de->td", mixed_rows, out_full, preferred_element_type=jnp.float32
    )
    summed = lax.psum(partial_value.astype(jnp.bfloat16), "tensor").astype(jnp.float32)
    post_factor = lax.rsqrt(jnp.mean(summed * summed, axis=1, keepdims=True) + norm_eps)
    layer_full = (student_f + summed * post_factor * post_gain).astype(jnp.bfloat16)
    loss_grad = loss_scale * (layer_full.astype(jnp.float32) - target.astype(jnp.float32))
    scaled = post_gain * loss_grad
    along_sum = jnp.mean(summed * scaled, axis=1, keepdims=True)
    pre_grad = (
        post_factor * scaled - summed * post_factor * post_factor * post_factor * along_sum
    ).astype(jnp.bfloat16)
    mixed_grad = jnp.dot(pre_grad, out_full, preferred_element_type=jnp.float32).astype(
        jnp.bfloat16
    )
    grouped_g = mixed_grad.reshape(tok_count, local_groups, group_size, HD)
    prob_grad = jnp.einsum(
        "tgad,kgd->gatk", grouped_g, grouped_v, preferred_element_type=jnp.float32
    )
    score_grad = (
        attn_probs * (prob_grad - jnp.sum(attn_probs * prob_grad, axis=3, keepdims=True))
    ).astype(jnp.bfloat16)
    rotated_grad = (
        jnp.einsum(
            "gatk,kgd->tgad", score_grad, grouped_k, preferred_element_type=jnp.float32
        ).reshape(tok_count, query_cols)
        * score_scale
    )
    query_pre = rotate(rotated_grad, cos_table, sin_table, -1.0).astype(jnp.bfloat16)
    query_term = jnp.einsum("td,te->de", normed, query_pre, preferred_element_type=jnp.float32)
    out_term = jnp.einsum("td,te->de", pre_grad, mixed_rows, preferred_element_type=jnp.float32)
    grad_owned = lax.psum_scatter(
        jnp.concatenate([query_term, out_term], axis=1).astype(jnp.bfloat16),
        ("sec", "dp"),
        scatter_dimension=0,
        tiled=True,
    ).astype(jnp.float32)
    layer_share = lax.dynamic_slice_in_dim(
        layer_full, lax.axis_index("tensor") * share_cols, share_cols, 1
    )
    return (layer_share[None], grad_owned[:, :query_cols], grad_owned[:, query_cols:])


def solution(mesh):
    in_specs = (
        P("sec", "dp", None),
        P("sec", "dp", None),
        P(),
        P(),
        P(("sec", "dp"), "tensor"),
        P(("sec", "dp"), "tensor"),
        P(("sec", "dp"), "tensor"),
        P(("sec", "dp"), "tensor"),
    )
    out_specs = (P("sec", "dp", "tensor"), P(("sec", "dp"), "tensor"), P(("sec", "dp"), "tensor"))
    return jax.shard_map(shards, mesh=mesh, in_specs=in_specs, out_specs=out_specs, check_vma=False)
```

profile of v0, /device:TPU:2, one launch (start us, length us, event | category | flops | bytes accessed | tf_op | source)
XLA Modules:
  0.0 628.8 jit_solution(17924069632204809534)
XLA Ops:
  7.2 0.7 all-gather.7.cloned.1.call-update
  8.0 0.7 all-gather.5.cloned.1.call-update
  8.7 0.7 all-gather.9.cloned.1.call-update
  9.4 0.5 all-gather.11.cloned.1.call-update
  10.1 3.7 fusion.9
  13.8 1.0 broadcast_multiply_fusion
  14.8 1.2 compare_and_fusion
  16.0 53.6 %all-gather.7.cloned.1.call-done = bf16[5376,256]{1,0:T(8,128)(2,1)} async-done(((bf16[168,256]{1,0:T(8,128)(2,1)}), bf16[5376,256]{1,0:T(8,128)(2,1)}) %all-gather.7.cloned.1.call-update) | async-done | bytes 2752528 | tf_op jit(solution)/shard_map/all_gather | solution.py:72
  69.6 5.4 fusion.50
  75.0 1.2 fusion.66
  76.2 2.1 collective-permute-start.3
  78.4 4.0 collective-permute-start.2
  82.4 53.2 %all-gather.5.cloned.1.call-done = bf16[5376,256]{1,0:T(8,128)(2,1)} async-done(((bf16[168,256]{1,0:T(8,128)(2,1)}), bf16[5376,256]{1,0:T(8,128)(2,1)}) %all-gather.5.cloned.1.call-update) | async-done | bytes 2752528 | tf_op jit(solution)/shard_map/all_gather | solution.py:73
  135.6 5.0 fusion.53
  140.7 2.1 collective-permute-start.1
  142.8 4.3 collective-permute-start
  147.1 57.4 %all-gather.9.cloned.1.call-done = bf16[5376,512]{1,0:T(8,128)(2,1)} async-done(((bf16[168,512]{1,0:T(8,128)(2,1)}), bf16[5376,512]{1,0:T(8,128)(2,1)}) %all-gather.9.cloned.1.call-update) | async-done | bytes 5505040 | tf_op jit(solution)/shard_map/all_gather | solution.py:71
  204.5 8.3 %copy.30 = bf16[512,5376]{1,0:T(8,128)(2,1)} copy(bf16[512,5376]{0,1:T(8,128)(2,1)} %bitcast.134) | data formatting | bytes 11010048 | tf_op jit(solution)/shard_map/dot_general | solution.py:89
  212.8 7.0 %fusion.22 = f32[512,2,256]{0,2,1:T(8,128)S(1)} fusion(bf16[2,256,5376]{2,1,0:T(8,128)(2,1)} %bitcast.135, bf16[1,512,5376]{2,1,0:T(8,128)(2,1)} %param.8, f32[5376]{0:T(1024)S(1)} %copy-done.4, f32[512]{0:T(512)S(1)} %add_rsqrt_fusion.1), kind=kOutput, calls=%fused_computation.36 | convolution fusion | flops 2829582336 | bytes 12082176 | tf_op jit(solution)/shard_map/dot_general | solution.py:89
  219.7 0.2 subtract_convert_fusion.1
  220.0 1.4 fusion.25
  221.4 1.5 fusion.21
  222.9 1.1 copy-done.2
  224.0 3.1 fusion.47
  227.1 39.8 %all-gather.11.cloned.1.call-done = bf16[5376,512]{1,0:T(8,128)(2,1)} async-done(((bf16[168,512]{1,0:T(8,128)(2,1)}), bf16[5376,512]{1,0:T(8,128)(2,1)}) %all-gather.11.cloned.1.call-update) | async-done | bytes 5505040 | tf_op jit(solution)/shard_map/all_gather | solution.py:74
  266.9 8.3 %convolution_convert_fusion.2 = bf16[512,5376]{1,0:T(8,128)(2,1)} fusion(bf16[512,512]{0,1:T(8,128)(2,1)} %bitcast.139, bf16[5376,512]{1,0:T(8,128)(2,1)} %all-gather.11.cloned.1.call-done), kind=kOutput, calls=%fused_computation.26 | convolution fusion | flops 2821324800 | bytes 11534336 | tf_op jit(solution)/shard_map/te,de->td/dot_general | solution.py:129
  275.2 0.0 reduce-scatter.4.cloned.1.call-start
  275.3 1.6 collective-permute-start.4
  276.8 110.7 %all-reduce.2.cloned.1.call-done = bf16[512,5376]{1,0:T(8,128)(2,1)} async-done(((bf16[512,5376]{1,0:T(8,128)(2,1)}), bf16[512,5376]{1,0:T(8,128)(2,1)}) %all-reduce.2.cloned.1.call-update) | async-done | bytes 5505040 | tf_op jit(solution)/shard_map/psum | solution.py:132
  387.5 3.9 fusion.15
  391.4 5.3 collective-permute-done.4
  396.7 7.1 %fusion.16 = (f32[512]{0:T(512)S(1)}, bf16[512,5376]{1,0:T(8,128)(2,1)S(1)}) fusion(bf16[512,5376]{1,0:T(8,128)(2,1)S(1)} %copy-done, bf16[512,5376]{1,0:T(8,128)(2,1)} %collective-permute-done.4, f32[5376]{0:T(1024)S(1)} %broadcast_multiply_fusion.1, f32[5376]{0:T(1024)S(1)} %copy-done.3, f32[512]{0:T(512)S(1)} %add_rsqrt_fusion, bf16[1,512,5376]{2,1,0:T(8,128)(2,1)} %param.8), kind=kLoop, calls=%fused_computation.21 | loop fusion | flops 33029632 | bytes 22067200 | tf_op jit(solution)/shard_map/reduce_sum | solution.py:137
  403.8 8.0 %fusion.8 = bf16[512,5376]{1,0:T(8,128)(2,1)S(1)} fusion(bf16[512,5376]{1,0:T(8,128)(2,1)S(1)} %copy-done, bf16[512,5376]{1,0:T(8,128)(2,1)} %collective-permute-done.4, bf16[512,5376]{1,0:T(8,128)(2,1)S(1)} %get-tuple-element.13, f32[512]{0:T(512)S(1)} %broadcast_multiply_fusion.2, f32[5376]{0:T(1024)S(1)} %broadcast_multiply_fusion.1, f32[512]{0:T(512)S(1)} %add_rsqrt_fusion), kind=kLoop, calls=%fused_computation.13 | loop fusion | flops 33030144 | bytes 22045696 | tf_op jit(solution)/shard_map/convert_element_type | solution.py:140
  411.8 3.2 convolution_convert_fusion
  415.1 5.8 convolution_convert_fusion.3
  420.9 2.3 fusion.17
  423.2 2.7 fusion.44
  425.9 0.2 subtract_convert_fusion
  426.2 3.6 convolution_convert_fusion.1
  429.9 5.1 pad_maximum_fusion
  435.0 14.7 %copy.48 = bf16[5376,1024]{1,0:T(8,128)(2,1)} copy(bf16[5376,1024]{0,1:T(8,128)(2,1)} %pad_maximum_fusion) | data formatting | bytes 22020096
  449.7 2.3 constant_dynamic-slice_fusion
  452.0 1.5 copy.35
  453.5 165.0 %reduce-scatter.4.cloned.1.call-done = bf16[168,1024]{1,0:T(8,128)(2,1)} async-done(((bf16[5376,1024]{1,0:T(8,128)(2,1)}), bf16[168,1024]{1,0:T(8,128)(2,1)}) %reduce-scatter.4.cloned.1.call-update) | async-done | bytes 344080
  618.4 1.2 copy.49
  619.6 0.1 fusion.80
  619.7 0.9 copy.39
  620.6 0.9 copy.38
  (43 shorter events, 0.4 us)
Async XLA Ops:
  7.2 62.5 %copy-start.4 = (f32[5376]{0:T(1024)S(1)}, f32[5376]{0:T(1024)}, u32[]{:S(2)}) copy-start(f32[5376]{0:T(1024)} %param.10) | copy-start | bytes 64516
  7.2 62.5 %all-gather.7.cloned.1.call-start = ((), (), s32[]{:S(2)}) async-start(), calls=%async_computation.2 | async-start | bytes 2838528 | tf_op jit(solution)/shard_map/all_gather | solution.py:72
  7.9 127.7 %all-gather.5.cloned.1.call-start = ((), (), s32[]{:S(2)}) async-start(), calls=%async_computation.1 | async-start | bytes 2838528 | tf_op jit(solution)/shard_map/all_gather | solution.py:73
  8.7 195.8 %all-gather.9.cloned.1.call-start = ((), (), s32[]{:S(2)}) async-start(), calls=%async_computation.3 | async-start | bytes 5677056 | tf_op jit(solution)/shard_map/all_gather | solution.py:71
  9.4 257.5 %all-gather.11.cloned.1.call-start = ((), (), s32[]{:S(2)}) async-start(), calls=%async_computation.4 | async-start | bytes 5677056 | tf_op jit(solution)/shard_map/all_gather | solution.py:74
  10.0 377.5 %all-reduce.2.cloned.1.call-start = ((), (), s32[]{:S(2)}) async-start(), calls=%async_computation.5 | async-start | bytes 11010048 | tf_op jit(solution)/shard_map/psum | solution.py:132
  76.2 143.7 %collective-permute-start.3 = (bf16[512,256]{0,1:T(8,128)(2,1)S(1)}, bf16[512,256]{0,1:T(8,128)(2,1)S(1)}, u32[]{:S(2)}, u32[]{:S(2)}) collective-permute-start(bf16[512,256]{0,1:T(8,128)(2,1)S(1)} %maximum_bitcast_fusion.6), channel_id=1, source_target_pairs={{0,4},{4,8},{8,12},{12,16},{16,20},{20,24},{24,28},{28,32},{32,36}... | collective-permute-start | bytes 786440 | tf_op jit(solution)/shard_map/ppermute | solution.py:29
  78.4 141.6 %collective-permute-start.2 = (bf16[512,256]{0,1:T(8,128)(2,1)S(1)}, bf16[512,256]{0,1:T(8,128)(2,1)S(1)}, u32[]{:S(2)}, u32[]{:S(2)}) collective-permute-start(bf16[512,256]{0,1:T(8,128)(2,1)S(1)} %maximum_bitcast_fusion.6), channel_id=1, source_target_pairs={{0,8},{4,12},{8,16},{12,20},{16,24},{20,28},{24,32},{28,36},{32,40... | collective-permute-start | bytes 786440 | tf_op jit(solution)/shard_map/ppermute | solution.py:29
  140.7 82.2 %collective-permute-start.1 = (bf16[512,256]{1,0:T(8,128)(2,1)S(1)}, bf16[512,256]{1,0:T(8,128)(2,1)S(1)}, u32[]{:S(2)}, u32[]{:S(2)}) collective-permute-start(bf16[512,256]{1,0:T(8,128)(2,1)S(1)} %fusion.53), channel_id=1, source_target_pairs={{0,4},{4,8},{8,12},{12,16},{16,20},{20,24},{24,28},{28,32},{32,36}... | collective-permute-start | bytes 786440 | tf_op jit(solution)/shard_map/ppermute | solution.py:29
  142.8 80.1 %collective-permute-start = (bf16[512,256]{1,0:T(8,128)(2,1)S(1)}, bf16[512,256]{1,0:T(8,128)(2,1)S(1)}, u32[]{:S(2)}, u32[]{:S(2)}) collective-permute-start(bf16[512,256]{1,0:T(8,128)(2,1)S(1)} %fusion.53), channel_id=1, source_target_pairs={{0,8},{4,12},{8,16},{12,20},{16,24},{20,28},{24,32},{28,36},{32,40... | collective-permute-start | bytes 786440 | tf_op jit(solution)/shard_map/ppermute | solution.py:29
  221.4 2.7 copy-start.2
  266.9 9.9 %copy-start.3 = (f32[5376]{0:T(1024)S(1)}, f32[5376]{0:T(1024)}, u32[]{:S(2)}) copy-start(f32[5376]{0:T(1024)} %param.11) | copy-start | bytes 64516
  275.2 343.2 %reduce-scatter.4.cloned.1.call-start = ((), (), s32[]{:S(2)}) async-start(), calls=%async_computation.6 | async-start | bytes 11354112
  275.3 121.4 %collective-permute-start.4 = (bf16[512,5376]{1,0:T(8,128)(2,1)}, bf16[512,5376]{1,0:T(8,128)(2,1)}, u32[]{:S(2)}, u32[]{:S(2)}) collective-permute-start(bf16[512,5376]{1,0:T(8,128)(2,1)} %bitcast.138), channel_id=1, source_target_pairs={{0,64},{64,0},{1,65},{65,1},{2,66},{66,2},{3,67},{67,3},{4,68},{68... | collective-permute-start | bytes 16515080 | tf_op jit(solution)/shard_map/ppermute | solution.py:23
  387.5 9.2 %copy-start = (bf16[512,5376]{1,0:T(8,128)(2,1)S(1)}, bf16[512,5376]{1,0:T(8,128)(2,1)}, u32[]{:S(2)}) copy-start(bf16[512,5376]{1,0:T(8,128)(2,1)} %all-reduce.2.cloned.1.call-done) | copy-start | bytes 16515076
  403.8 8.0 %copy-start.1 = (bf16[512,5376]{1,0:T(8,128)(2,1)}, bf16[512,5376]{1,0:T(8,128)(2,1)S(1)}, u32[]{:S(2)}) copy-start(bf16[512,5376]{1,0:T(8,128)(2,1)S(1)} %get-tuple-element.13) | copy-start | bytes 16515076
  403.8 8.0 %copy-start.5 = (bf16[256,2,512]{2,0,1:T(8,128)(2,1)S(1)}, bf16[256,2,512]{2,0,1:T(8,128)(2,1)}, u32[]{:S(2)}) copy-start(bf16[256,2,512]{2,0,1:T(8,128)(2,1)} %fusion.47) | copy-start | bytes 1572868
  411.8 9.0 %slice-start.2 = ((s8[6291456]{0:T(1024)(128)(4,1)}), s8[4194304]{0:T(1024)(128)(4,1)S(1)}, s32[]{:S(2)}) async-start(s8[6291456]{0:T(1024)(128)(4,1)} %bitcast.132), calls=%async_computation.9 | async-start | bytes 8388608
  415.1 5.8 slice-start.3
  420.9 5.4 slice-start
  423.2 3.0 slice-start.1
Sparse Core Ops, SparseCore 0:
  9.7 59.8 all-gather.6
  71.3 64.2 all-gather.4
  137.3 67.1 all-gather.8
  206.1 60.8 all-gather.10
  275.3 112.1 all-reduce.1
  449.8 168.6 reduce-scatter.3
where the time goes:
time: 635 us; the launch traced here: 629 us
  waiting for transfers between devices  488 us (77%)
  matrix products  47.8 us (8%)
  other arithmetic  33.1 us (5%)
  local copies, waits for them, and re-layouts  31 us (5%)
  between operations  14.9 us (2%)
  starting transfers between devices  14.3 us (2%)
    unnamed x7, waiting for transfers between devices  168 us
    psum x1, waiting for transfers between devices, shards(): lax.psum(partial_value.astype(jnp.bfloat16), 'tensor').astype(jnp.float32)  111 us
    all_gather x1, waiting for transfers between devices, shards(): lax.all_gather(query_weight, ('sec', 'dp'), axis=0, tiled=True)  57.4 us
    all_gather x1, waiting for transfers between devices, shards(): lax.all_gather(key_weight, ('sec', 'dp'), axis=0, tiled=True)  53.6 us
    all_gather x1, waiting for transfers between devices, shards(): lax.all_gather(value_weight, ('sec', 'dp'), axis=0, tiled=True)  53.2 us
    all_gather x1, waiting for transfers between devices, shards(): lax.all_gather(out_weight, ('sec', 'dp'), axis=0, tiled=True)  39.8 us
    unnamed x24, local copies, waits for them, and re-layouts  18.9 us
  transfers between devices with their start and end apart: 11, of which 7 were waited for; matrix products, arithmetic and copies ran while one was open for 7% of the time, Pallas kernels for 0%

commit v1 on v0

--- a/solution.py
+++ b/solution.py
@@ -129,7 +129,9 @@
     partial_value = jnp.einsum(
         "te,de->td", mixed_rows, out_full, preferred_element_type=jnp.float32
     )
-    summed = lax.psum(partial_value.astype(jnp.bfloat16), "tensor").astype(jnp.float32)
+    summed = jnp.sum(lax.all_gather(partial_value.astype(jnp.bfloat16), "tensor"), axis=0).astype(
+        jnp.float32
+    )
     post_factor = lax.rsqrt(jnp.mean(summed * summed, axis=1, keepdims=True) + norm_eps)
     layer_full = (student_f + summed * post_factor * post_gain).astype(jnp.bfloat16)
     loss_grad = loss_scale * (layer_full.astype(jnp.float32) - target.astype(jnp.float32))

time: 635 us -> 730 us (1.15)
  waiting for transfers between devices: 488 us -> 563 us
  other arithmetic: 33.1 us -> 48.7 us
    all_gather x0 -> x1, waiting for transfers between devices: none -> 195 us  [shards(): lax.all_gather(partial_value.astype(jnp.bfloat16), 'tensor')]
    psum x1 -> x0, waiting for transfers between devices: 111 us -> none  [shards(): lax.psum(partial_value.astype(jnp.bfloat16), 'tensor').astype(jnp.float32)]
    reduce_sum x0 -> x1, other arithmetic: none -> 15.6 us  [shards(): jnp.sum(lax.all_gather(partial_value.astype(jnp.bfloat16), 'tensor'), axi...]
  transfers between devices with their start and end apart: 11 -> 11, of which waited for: 7 -> 6; matrix products, arithmetic and copies ran while one was open for 7% -> 9% of each run, Pallas kernels for 0% -> 0%
where the time goes in v1:
time: 730 us; the launch traced here: 720 us
  waiting for transfers between devices  563 us (77%)
  other arithmetic  48.7 us (7%)
  matrix products  48 us (7%)
  local copies, waits for them, and re-layouts  31.1 us (4%)
  between operations  14.7 us (2%)
  starting transfers between devices  13.9 us (2%)
    all_gather x1, waiting for transfers between devices, shards(): lax.all_gather(partial_value.astype(jnp.bfloat16), 'tensor')  195 us
    unnamed x7, waiting for transfers between devices  164 us
    all_gather x1, waiting for transfers between devices, shards(): lax.all_gather(query_weight, ('sec', 'dp'), axis=0, tiled=True)  57.4 us
    all_gather x1, waiting for transfers between devices, shards(): lax.all_gather(key_weight, ('sec', 'dp'), axis=0, tiled=True)  53.6 us
    all_gather x1, waiting for transfers between devices, shards(): lax.all_gather(value_weight, ('sec', 'dp'), axis=0, tiled=True)  53.4 us
    all_gather x1, waiting for transfers between devices, shards(): lax.all_gather(out_weight, ('sec', 'dp'), axis=0, tiled=True)  39.7 us
    unnamed x24, local copies, waits for them, and re-layouts  19.2 us
    reduce_sum x1, other arithmetic, shards(): jnp.sum(lax.all_gather(partial_value.astype(jnp.bfloat16), 'tensor'), axi...  15.6 us
  transfers between devices with their start and end apart: 11, of which 6 were waited for; matrix products, arithmetic and copies ran while one was open for 9% of the time, Pallas kernels for 0%

profile of v1, /device:TPU:2, one launch (start us, length us, event | category | flops | bytes accessed | tf_op | source)
XLA Modules:
  0.0 719.5 jit_solution(14371583864398605268)
XLA Ops:
  7.2 0.7 all-gather.9.cloned.1.call-update
  8.0 0.7 all-gather.7.cloned.1.call-update
  8.7 0.7 all-gather.11.cloned.1.call-update
  9.4 0.5 all-gather.13.cloned.1.call-update
  10.1 3.7 fusion.9
  13.8 1.0 broadcast_multiply_fusion
  14.8 1.2 compare_and_fusion
  16.0 53.6 %all-gather.9.cloned.1.call-done = bf16[5376,256]{1,0:T(8,128)(2,1)} async-done(((bf16[168,256]{1,0:T(8,128)(2,1)}), bf16[5376,256]{1,0:T(8,128)(2,1)}) %all-gather.9.cloned.1.call-update) | async-done | bytes 2752528 | tf_op jit(solution)/shard_map/all_gather | solution.py:72
  69.6 5.4 fusion.50
  75.0 1.2 fusion.66
  76.2 4.0 collective-permute-start.2
  80.2 1.9 collective-permute-start.3
  82.1 53.4 %all-gather.7.cloned.1.call-done = bf16[5376,256]{1,0:T(8,128)(2,1)} async-done(((bf16[168,256]{1,0:T(8,128)(2,1)}), bf16[5376,256]{1,0:T(8,128)(2,1)}) %all-gather.7.cloned.1.call-update) | async-done | bytes 2752528 | tf_op jit(solution)/shard_map/all_gather | solution.py:73
  135.5 5.0 fusion.53
  140.6 4.0 collective-permute-start
  144.6 2.3 collective-permute-start.1
  146.9 57.4 %all-gather.11.cloned.1.call-done = bf16[5376,512]{1,0:T(8,128)(2,1)} async-done(((bf16[168,512]{1,0:T(8,128)(2,1)}), bf16[5376,512]{1,0:T(8,128)(2,1)}) %all-gather.11.cloned.1.call-update) | async-done | bytes 5505040 | tf_op jit(solution)/shard_map/all_gather | solution.py:71
  204.3 8.0 %copy.21 = bf16[512,5376]{1,0:T(8,128)(2,1)} copy(bf16[512,5376]{0,1:T(8,128)(2,1)} %bitcast.136) | data formatting | bytes 11010048 | tf_op jit(solution)/shard_map/dot_general | solution.py:89
  212.4 7.0 fusion.22
  219.3 0.2 subtract_convert_fusion.1
  219.6 1.4 fusion.25
  221.0 1.5 fusion.21
  222.5 1.1 copy-done.2
  223.6 3.1 fusion.47
  226.7 39.7 %all-gather.13.cloned.1.call-done = bf16[5376,512]{1,0:T(8,128)(2,1)} async-done(((bf16[168,512]{1,0:T(8,128)(2,1)}), bf16[5376,512]{1,0:T(8,128)(2,1)}) %all-gather.13.cloned.1.call-update) | async-done | bytes 5505040 | tf_op jit(solution)/shard_map/all_gather | solution.py:74
  266.5 8.2 %convolution_convert_fusion.2 = bf16[512,5376]{1,0:T(8,128)(2,1)} fusion(bf16[512,512]{0,1:T(8,128)(2,1)} %bitcast.141, bf16[5376,512]{1,0:T(8,128)(2,1)} %all-gather.13.cloned.1.call-done), kind=kOutput, calls=%fused_computation.26 | convolution fusion | flops 2821324800 | bytes 11534336 | tf_op jit(solution)/shard_map/te,de->td/dot_general | solution.py:129
  274.8 1.5 collective-permute-start.4
  276.3 195.3 %all-gather.15.cloned.1.call-done = bf16[2048,5376]{1,0:T(8,128)(2,1)} async-done(((bf16[512,5376]{1,0:T(8,128)(2,1)}), bf16[2048,5376]{1,0:T(8,128)(2,1)}) %all-gather.15.cloned.1.call-update) | async-done | bytes 22020112 | tf_op jit(solution)/shard_map/all_gather | solution.py:132
  471.5 15.6 %reduce_sum.59 = bf16[512,5376]{1,0:T(8,128)(2,1)} reduce(bf16[4,512,5376]{2,1,0:T(8,128)(2,1)} %bitcast.131, bf16[]{:T(256)} %constant.46.clone.1), dimensions={0}, to_apply=%region_3.4 | reduce | flops 8257536 | bytes 27525122 | tf_op jit(solution)/shard_map/reduce_sum | solution.py:132
  487.1 3.9 fusion.15
  491.0 0.3 copy-done
  491.3 7.1 fusion.16
  498.4 8.0 %fusion.8 = bf16[512,5376]{1,0:T(8,128)(2,1)S(1)} fusion(bf16[512,5376]{1,0:T(8,128)(2,1)S(1)} %copy-done, bf16[512,5376]{1,0:T(8,128)(2,1)} %collective-permute-done.4, bf16[512,5376]{1,0:T(8,128)(2,1)S(1)} %get-tuple-element.10, f32[512]{0:T(512)S(1)} %broadcast_multiply_fusion.2, f32[5376]{0:T(1024)S(1)} %broadcast_multiply_fusion.1, f32[512]{0:T(512)S(1)} %add_rsqrt_fusion), kind=kLoop, calls=%fused_computation.13 | loop fusion | flops 33030144 | bytes 22045696 | tf_op jit(solution)/shard_map/convert_element_type | solution.py:142
  506.4 3.4 convolution_convert_fusion
  509.9 5.8 convolution_convert_fusion.3
  515.7 2.3 fusion.17
  518.1 2.7 fusion.44
  520.8 0.2 subtract_convert_fusion
  521.1 3.6 convolution_convert_fusion.1
  524.7 5.1 pad_maximum_fusion
  529.8 14.7 %copy.39 = bf16[5376,1024]{1,0:T(8,128)(2,1)} copy(bf16[5376,1024]{0,1:T(8,128)(2,1)} %pad_maximum_fusion) | data formatting | bytes 22020096
  544.5 2.3 constant_dynamic-slice_fusion
  546.8 1.5 copy.26
  548.3 161.0 %reduce-scatter.4.cloned.1.call-done = bf16[168,1024]{1,0:T(8,128)(2,1)} async-done(((bf16[5376,1024]{1,0:T(8,128)(2,1)}), bf16[168,1024]{1,0:T(8,128)(2,1)}) %reduce-scatter.4.cloned.1.call-update) | async-done | bytes 344080
  709.4 1.2 copy.40
  710.5 0.1 fusion.80
  710.6 0.9 copy.29
  711.5 0.9 copy.30
  (44 shorter events, 0.4 us)
Async XLA Ops:
  7.2 62.5 %copy-start.4 = (f32[5376]{0:T(1024)S(1)}, f32[5376]{0:T(1024)}, u32[]{:S(2)}) copy-start(f32[5376]{0:T(1024)} %param.10) | copy-start | bytes 64516
  7.2 62.5 %all-gather.9.cloned.1.call-start = ((), (), s32[]{:S(2)}) async-start(), calls=%async_computation.2 | async-start | bytes 2838528 | tf_op jit(solution)/shard_map/all_gather | solution.py:72
  7.9 127.6 %all-gather.7.cloned.1.call-start = ((), (), s32[]{:S(2)}) async-start(), calls=%async_computation.1 | async-start | bytes 2838528 | tf_op jit(solution)/shard_map/all_gather | solution.py:73
  8.7 195.7 %all-gather.11.cloned.1.call-start = ((), (), s32[]{:S(2)}) async-start(), calls=%async_computation.3 | async-start | bytes 5677056 | tf_op jit(solution)/shard_map/all_gather | solution.py:71
  9.4 257.1 %all-gather.13.cloned.1.call-start = ((), (), s32[]{:S(2)}) async-start(), calls=%async_computation.4 | async-start | bytes 5677056 | tf_op jit(solution)/shard_map/all_gather | solution.py:74
  10.0 461.6 %all-gather.15.cloned.1.call-start = ((), (), s32[]{:S(2)}) async-start(), calls=%async_computation.5 | async-start | bytes 27525120 | tf_op jit(solution)/shard_map/all_gather | solution.py:132
  76.2 143.3 %collective-permute-start.2 = (bf16[512,256]{0,1:T(8,128)(2,1)S(1)}, bf16[512,256]{0,1:T(8,128)(2,1)S(1)}, u32[]{:S(2)}, u32[]{:S(2)}) collective-permute-start(bf16[512,256]{0,1:T(8,128)(2,1)S(1)} %maximum_bitcast_fusion.6), channel_id=1, source_target_pairs={{0,8},{4,12},{8,16},{12,20},{16,24},{20,28},{24,32},{28,36},{32,40... | collective-permute-start | bytes 786440 | tf_op jit(solution)/shard_map/ppermute | solution.py:29
  80.2 139.3 %collective-permute-start.3 = (bf16[512,256]{0,1:T(8,128)(2,1)S(1)}, bf16[512,256]{0,1:T(8,128)(2,1)S(1)}, u32[]{:S(2)}, u32[]{:S(2)}) collective-permute-start(bf16[512,256]{0,1:T(8,128)(2,1)S(1)} %maximum_bitcast_fusion.6), channel_id=1, source_target_pairs={{0,4},{4,8},{8,12},{12,16},{16,20},{20,24},{24,28},{28,32},{32,36}... | collective-permute-start | bytes 786440 | tf_op jit(solution)/shard_map/ppermute | solution.py:29
  140.6 81.9 %collective-permute-start = (bf16[512,256]{1,0:T(8,128)(2,1)S(1)}, bf16[512,256]{1,0:T(8,128)(2,1)S(1)}, u32[]{:S(2)}, u32[]{:S(2)}) collective-permute-start(bf16[512,256]{1,0:T(8,128)(2,1)S(1)} %fusion.53), channel_id=1, source_target_pairs={{0,8},{4,12},{8,16},{12,20},{16,24},{20,28},{24,32},{28,36},{32,40... | collective-permute-start | bytes 786440 | tf_op jit(solution)/shard_map/ppermute | solution.py:29
  144.6 77.9 %collective-permute-start.1 = (bf16[512,256]{1,0:T(8,128)(2,1)S(1)}, bf16[512,256]{1,0:T(8,128)(2,1)S(1)}, u32[]{:S(2)}, u32[]{:S(2)}) collective-permute-start(bf16[512,256]{1,0:T(8,128)(2,1)S(1)} %fusion.53), channel_id=1, source_target_pairs={{0,4},{4,8},{8,12},{12,16},{16,20},{20,24},{24,28},{28,32},{32,36}... | collective-permute-start | bytes 786440 | tf_op jit(solution)/shard_map/ppermute | solution.py:29
  221.0 2.7 copy-start.2
  266.5 9.8 %copy-start.3 = (f32[5376]{0:T(1024)S(1)}, f32[5376]{0:T(1024)}, u32[]{:S(2)}) copy-start(f32[5376]{0:T(1024)} %param.11) | copy-start | bytes 64516
  274.7 434.6 %reduce-scatter.4.cloned.1.call-start = ((), (), s32[]{:S(2)}) async-start(), calls=%async_computation.6 | async-start | bytes 11354112
  274.8 216.2 %collective-permute-start.4 = (bf16[512,5376]{1,0:T(8,128)(2,1)}, bf16[512,5376]{1,0:T(8,128)(2,1)}, u32[]{:S(2)}, u32[]{:S(2)}) collective-permute-start(bf16[512,5376]{1,0:T(8,128)(2,1)} %bitcast.140), channel_id=1, source_target_pairs={{0,64},{64,0},{1,65},{65,1},{2,66},{66,2},{3,67},{67,3},{4,68},{68... | collective-permute-start | bytes 16515080 | tf_op jit(solution)/shard_map/ppermute | solution.py:23
  487.1 4.2 copy-start
  498.4 8.0 %copy-start.1 = (bf16[512,5376]{1,0:T(8,128)(2,1)}, bf16[512,5376]{1,0:T(8,128)(2,1)S(1)}, u32[]{:S(2)}) copy-start(bf16[512,5376]{1,0:T(8,128)(2,1)S(1)} %get-tuple-element.10) | copy-start | bytes 16515076
  498.4 8.0 %copy-start.5 = (bf16[256,2,512]{2,0,1:T(8,128)(2,1)S(1)}, bf16[256,2,512]{2,0,1:T(8,128)(2,1)}, u32[]{:S(2)}) copy-start(bf16[256,2,512]{2,0,1:T(8,128)(2,1)} %fusion.47) | copy-start | bytes 1572868
  506.4 9.2 %slice-start.2 = ((s8[6291456]{0:T(1024)(128)(4,1)}), s8[4194304]{0:T(1024)(128)(4,1)S(1)}, s32[]{:S(2)}) async-start(s8[6291456]{0:T(1024)(128)(4,1)} %bitcast.134), calls=%async_computation.9 | async-start | bytes 8388608
  509.9 5.8 slice-start.3
  515.7 5.4 slice-start
  518.0 3.0 slice-start.1
Sparse Core Ops, SparseCore 0:
  9.7 59.8 all-gather.8
  71.3 64.1 all-gather.6
  137.2 67.0 all-gather.10
  205.9 60.5 all-gather.12
  274.8 196.6 all-gather.14
  544.6 164.6 reduce-scatter.3
